TPU v7x, 256 devices: a whole 4x4x8 slice. The times are simulated.
256 devices in a mesh: dp: 4 (over x), state: 64 (over y, z, core).
Axes of the slice: x: 4, y: 4, z: 8, core: 2. Of those that a mesh axis runs over, the one named last changes fastest.
Arguments:
- alpha_init: bfloat16 [32, 1024, 1024], P('dp', 'state'), may hold values from 0.099609375 to 4
- tokens: int32 [32, 3], P('dp'), may hold values from 0 to 511
- trans_rows: bfloat16 [1024, 1024], replicated, may hold values from 5e-05 to 1.11, as said below
- trans_cols: bfloat16 [1024, 1024], replicated, may hold values from 5e-05 to 1.11, as said below
- emit_rows: bfloat16 [512, 1024], replicated, may hold values from 0.001 to 1, as said below
- emit_cols: bfloat16 [512, 1024], replicated, may hold values from 0.001 to 1, as said below
- backward: bfloat16 [3, 32, 1024, 1024], P(None, 'dp', None, 'state'), may hold values from 0.2 to 32, as said below
Outputs:
- alpha_final: bfloat16 [32, 1024, 1024], P('dp', 'state')
- counts_rows: float32 [1024, 1024], P(None, ('dp', 'state'))
- counts_cols: float32 [1024, 1024], P(None, ('dp', 'state'))
- loglik: float32 [32], P('dp')
Inputs may be any that keep to these rules, and one draw needn't show every extreme that they name: `trans_rows`: positive transition weights. `trans_cols`: positive transition weights. `emit_rows`: positive emission weights. `emit_cols`: positive emission weights. Positive backward weights.
All inputs are finite; a program needn't handle non-finite values.
Results may differ from a plain program's by a relative error of at most 0.0046.
Values may be sent and summed in bfloat16 or wider, within the bound.
No kernel may reach another device: no remote copies, remote signals or barrier semaphores. Data moves between devices by JAX's collectives and lax.ppermute only.
A program may use at most 128 MiB of HBM per device.

v0:
```python
import jax
import jax.numpy as jnp
from jax import lax
from jax.sharding import PartitionSpec as P

STEPS = 3


def on_device(alpha_init, tokens, trans_rows, trans_cols, emit_rows, emit_cols, backward):
    f32 = jnp.float32
    groups = lax.axis_size("state")
    seq_dev = alpha_init.shape[0]
    width_rows = trans_rows.shape[0]
    width_cols = trans_cols.shape[0]
    cols_dev = width_cols // groups
    offset = lax.axis_index("state") * cols_dev
    alpha = alpha_init
    sums_rows = jnp.zeros((width_rows, width_rows), f32)
    sums_cols = jnp.zeros((width_cols, width_cols), f32)
    loglik = jnp.zeros((seq_dev,), f32)
    for step in range(STEPS):
        tok = tokens[:, step]
        first = jnp.take(emit_rows, tok, axis=0).astype(f32)
        second_all = jnp.take(emit_cols, tok, axis=0)
        second = lax.dynamic_slice_in_dim(second_all, offset, cols_dev, 1).astype(f32)
        mixed = jnp.einsum("sij,jk->sik", alpha, trans_cols, preferred_element_type=f32).astype(
            jnp.bfloat16
        )
        mixed_cols = lax.all_to_all(mixed, "state", split_axis=2, concat_axis=1, tiled=True)
        moved = jnp.einsum("sik,il->slk", mixed_cols, trans_rows, preferred_element_type=f32)
        emission = first[:, :, None] * second[:, None, :]
        scaled = moved * emission
        total = lax.psum(jnp.sum(scaled, axis=(1, 2)), "state")
        norm = total / (width_rows * width_cols)
        weight = (emission * backward[step].astype(f32) / norm[:, None, None]).astype(jnp.bfloat16)
        pulled = jnp.einsum("il,slk->sik", trans_rows, weight, preferred_element_type=f32).astype(
            jnp.bfloat16
        )
        pulled_local = lax.all_to_all(pulled, "state", split_axis=1, concat_axis=2, tiled=True)
        sums_rows = sums_rows + jnp.einsum(
            "sik,slk->il", mixed_cols, weight, preferred_element_type=f32
        )
        sums_cols = sums_cols + jnp.einsum(
            "sij,sik->jk", alpha, pulled_local, preferred_element_type=f32
        )
        loglik = loglik + jnp.log(norm)
        fresh = (scaled / norm[:, None, None]).astype(jnp.bfloat16)
        alpha = lax.all_to_all(fresh, "state", split_axis=1, concat_axis=2, tiled=True)
    factor = 1.0 / (seq_dev * lax.axis_size("dp") * STEPS)
    terms_rows = trans_rows.astype(f32) * sums_rows * factor
    terms_cols = trans_cols.astype(f32) * sums_cols * factor
    counts_rows, counts_cols = (
        lax.psum_scatter(terms_rows, ("dp", "state"), scatter_dimension=1, tiled=True),
        lax.psum_scatter(terms_cols, ("dp", "state"), scatter_dimension=1, tiled=True),
    )
    return (alpha, counts_rows, counts_cols, loglik)


def solution(mesh):
    return jax.shard_map(
        on_device,
        mesh=mesh,
        in_specs=(
            P("dp", "state", None),
            P("dp", None),
            P(),
            P(),
            P(),
            P(),
            P(None, "dp", None, "state"),
        ),
        out_specs=(
            P("dp", "state", None),
            P(None, ("dp", "state")),
            P(None, ("dp", "state")),
            P("dp"),
        ),
        check_vma=False,
    )
```

profile of v0, /device:TPU:2, one launch (start us, length us, event | category | flops | bytes accessed | tf_op | source)
XLA Modules:
  0.0 962.1 jit_solution(3449522075632876979)
XLA Ops:
  11.0 2.9 reshape.105
  14.0 12.1 %all-to-all-start = ((bf16[64,2,1024]{2,1,0:T(2,128)(2,1)}), bf16[64,2,1024]{2,1,0:T(2,128)(2,1)S(1)}, u32[]{:S(2)}, u32[]{:S(2)}) async-start(bf16[64,2,1024]{2,1,0:T(2,128)(2,1)} %reshape.105), calls=%async_computation | async-start | bytes 524288 | tf_op jit(solution)/shard_map/all_to_all | solution.py:29
  28.8 9.3 all-to-all-done
  42.2 4.8 all_to_all.120
  48.3 125.5 %psum.21 = f32[8]{0:T(128)S(1)} all-reduce(f32[8]{0:T(128)S(1)} %get-tuple-element.19), channel_id=1, replica_groups=mesh['dp'=4,'state'=64] {'state'}, use_global_device_ids=true, to_apply=%region_1.3 | all-reduce | flops 8 | bytes 64 | tf_op jit(solution)/shard_map/psum | solution.py:33
  178.2 2.9 reshape.107
  181.1 6.0 all-to-all-start.1
  190.4 8.6 all-to-all-done.1
  199.0 2.8 reshape.108
  204.5 4.8 all_to_all.124
  212.3 4.4 reshape.109
  216.6 6.0 all-to-all-start.2
  227.3 3.9 copy.51
  236.3 4.4 reshape.117
  240.7 10.6 %all-to-all-start.6 = ((bf16[64,2,1024]{2,1,0:T(2,128)(2,1)}), bf16[64,2,1024]{2,1,0:T(2,128)(2,1)}, u32[]{:S(2)}, u32[]{:S(2)}) async-start(bf16[64,2,1024]{2,1,0:T(2,128)(2,1)} %reshape.117), calls=%async_computation.6 | async-start | bytes 524288 | tf_op jit(solution)/shard_map/all_to_all | solution.py:39
  253.7 4.3 copy.41
  258.0 4.7 all_to_all.128
  264.8 128.9 %psum.22 = f32[8]{0:T(128)S(1)} all-reduce(f32[8]{0:T(128)S(1)} %get-tuple-element.21), channel_id=1, replica_groups=mesh['dp'=4,'state'=64] {'state'}, use_global_device_ids=true, to_apply=%region_3.5 | all-reduce | flops 8 | bytes 64 | tf_op jit(solution)/shard_map/psum | solution.py:33
  394.5 3.3 copy.42
  397.9 4.4 reshape.111
  402.3 4.8 all-to-all-start.3
  407.1 3.7 fusion.83
  410.8 3.6 reshape.118
  414.5 4.3 copy.55
  418.8 5.3 all_to_all.144
  429.2 4.4 reshape.119
  433.5 10.7 %all-to-all-start.7 = ((bf16[64,2,1024]{2,1,0:T(2,128)(2,1)}), bf16[64,2,1024]{2,1,0:T(2,128)(2,1)S(1)}, u32[]{:S(2)}, u32[]{:S(2)}) async-start(bf16[64,2,1024]{2,1,0:T(2,128)(2,1)} %reshape.119), calls=%async_computation.7 | async-start | bytes 524288 | tf_op jit(solution)/shard_map/all_to_all | solution.py:39
  444.2 3.7 fusion.88
  450.3 4.3 copy.44
  454.6 4.7 all_to_all.132
  461.4 2.9 reshape.113
  464.3 10.9 %all-to-all-start.4 = ((bf16[64,2,1024]{2,1,0:T(2,128)(2,1)}), bf16[64,2,1024]{2,1,0:T(2,128)(2,1)S(1)}, u32[]{:S(2)}, u32[]{:S(2)}) async-start(bf16[64,2,1024]{2,1,0:T(2,128)(2,1)} %reshape.113), calls=%async_computation.4 | async-start | bytes 524288 | tf_op jit(solution)/shard_map/all_to_all | solution.py:29
  475.2 3.7 fusion.80
  480.3 2.7 copy.58
  483.1 4.7 all_to_all.148
  494.7 4.8 all_to_all.136
  500.8 129.1 %psum.23 = f32[8]{0:T(128)S(1)} all-reduce(f32[8]{0:T(128)S(1)} %get-tuple-element.23), channel_id=1, replica_groups=mesh['dp'=4,'state'=64] {'state'}, use_global_device_ids=true, to_apply=%region_5.7 | all-reduce | flops 8 | bytes 64 | tf_op jit(solution)/shard_map/psum | solution.py:33
  634.7 4.4 reshape.121
  639.1 4.8 all-to-all-start.8
  643.9 6.5 fusion.4
  650.4 5.4 all-to-all-done.8
  660.0 4.8 all_to_all.152
  664.8 6.4 fusion.2
  674.0 2.9 reshape.115
  677.0 6.3 all-to-all-start.5
  683.2 13.2 %all-to-all-done.5 = bf16[64,2,1024]{2,1,0:T(2,128)(2,1)S(1)} async-done(((bf16[64,2,1024]{2,1,0:T(2,128)(2,1)}), bf16[64,2,1024]{2,1,0:T(2,128)(2,1)S(1)}, u32[]{:S(2)}, u32[]{:S(2)}) %all-to-all-start.5) | async-done | bytes 262176 | tf_op jit(solution)/shard_map/all_to_all | solution.py:48
  700.6 5.4 all_to_all.140
  706.0 246.3 %all-reduce.5.cloned.1.call-done = (f32[1024,1024]{0,1:T(8,128)}, f32[1024,1024]{0,1:T(8,128)}) async-done(((f32[1024,1024]{0,1:T(8,128)}, f32[1024,1024]{0,1:T(8,128)}), (f32[1024,1024]{0,1:T(8,128)}, f32[1024,1024]{0,1:T(8,128)})) %all-reduce.5.cloned.1.call-update) | async-done | bytes 8388624
  (81 shorter events, 77.7 us)
Async XLA Ops:
  7.2 20.9 %copy-start = (bf16[512,1024]{1,0:T(8,128)(2,1)S(1)}, bf16[512,1024]{1,0:T(8,128)(2,1)}, u32[]{:S(2)}) copy-start(bf16[512,1024]{1,0:T(8,128)(2,1)} %param.13) | copy-start | bytes 3145732
  9.4 16.7 %copy-start.9 = (s32[8,3]{0,1:T(4,128)S(1)}, s32[8,3]{0,1:T(4,128)}, u32[]{:S(2)}) copy-start(s32[8,3]{0,1:T(4,128)} %param.10) | copy-start | bytes 292
  14.0 24.1 %all-to-all-start = ((bf16[64,2,1024]{2,1,0:T(2,128)(2,1)}), bf16[64,2,1024]{2,1,0:T(2,128)(2,1)S(1)}, u32[]{:S(2)}, u32[]{:S(2)}) async-start(bf16[64,2,1024]{2,1,0:T(2,128)(2,1)} %reshape.105), calls=%async_computation | async-start | bytes 524288 | tf_op jit(solution)/shard_map/all_to_all | solution.py:29
  42.2 4.9 copy-start.3
  181.1 17.9 %all-to-all-start.1 = ((bf16[64,2,1024]{2,1,0:T(2,128)(2,1)}), bf16[64,2,1024]{2,1,0:T(2,128)(2,1)}, u32[]{:S(2)}, u32[]{:S(2)}) async-start(bf16[64,2,1024]{2,1,0:T(2,128)(2,1)} %reshape.107), calls=%async_computation.1 | async-start | bytes 524288 | tf_op jit(solution)/shard_map/all_to_all | solution.py:48
  204.5 4.9 copy-start.2
  216.6 24.0 %all-to-all-start.2 = ((bf16[64,2,1024]{2,1,0:T(2,128)(2,1)}), bf16[64,2,1024]{2,1,0:T(2,128)(2,1)S(1)}, u32[]{:S(2)}, u32[]{:S(2)}) async-start(bf16[64,2,1024]{2,1,0:T(2,128)(2,1)} %reshape.109), calls=%async_computation.2 | async-start | bytes 524288 | tf_op jit(solution)/shard_map/all_to_all | solution.py:29
  240.7 161.6 %all-to-all-start.6 = ((bf16[64,2,1024]{2,1,0:T(2,128)(2,1)}), bf16[64,2,1024]{2,1,0:T(2,128)(2,1)}, u32[]{:S(2)}, u32[]{:S(2)}) async-start(bf16[64,2,1024]{2,1,0:T(2,128)(2,1)} %reshape.117), calls=%async_computation.6 | async-start | bytes 524288 | tf_op jit(solution)/shard_map/all_to_all | solution.py:39
  402.3 31.3 %all-to-all-start.3 = ((bf16[64,2,1024]{2,1,0:T(2,128)(2,1)}), bf16[64,2,1024]{2,1,0:T(2,128)(2,1)S(1)}, u32[]{:S(2)}, u32[]{:S(2)}) async-start(bf16[64,2,1024]{2,1,0:T(2,128)(2,1)} %reshape.111), calls=%async_computation.3 | async-start | bytes 524288 | tf_op jit(solution)/shard_map/all_to_all | solution.py:48
  426.7 17.6 %copy-start.8 = (bf16[8,16,1024]{2,1,0:T(8,128)(2,1)S(1)}, bf16[8,16,1024]{2,1,0:T(8,128)(2,1)}, u32[]{:S(2)}) copy-start(bf16[8,16,1024]{2,1,0:T(8,128)(2,1)} %param.9) | copy-start | bytes 786436
  433.5 30.8 %all-to-all-start.7 = ((bf16[64,2,1024]{2,1,0:T(2,128)(2,1)}), bf16[64,2,1024]{2,1,0:T(2,128)(2,1)S(1)}, u32[]{:S(2)}, u32[]{:S(2)}) async-start(bf16[64,2,1024]{2,1,0:T(2,128)(2,1)} %reshape.119), calls=%async_computation.7 | async-start | bytes 524288 | tf_op jit(solution)/shard_map/all_to_all | solution.py:39
  464.3 26.2 %all-to-all-start.4 = ((bf16[64,2,1024]{2,1,0:T(2,128)(2,1)}), bf16[64,2,1024]{2,1,0:T(2,128)(2,1)S(1)}, u32[]{:S(2)}, u32[]{:S(2)}) async-start(bf16[64,2,1024]{2,1,0:T(2,128)(2,1)} %reshape.113), calls=%async_computation.4 | async-start | bytes 524288 | tf_op jit(solution)/shard_map/all_to_all | solution.py:29
  494.7 4.9 copy-start.4
  632.2 11.7 %copy-start.5 = (bf16[1024,1024]{0,1:T(8,128)(2,1)S(1)}, bf16[1024,1024]{0,1:T(8,128)(2,1)}, u32[]{:S(2)}) copy-start(bf16[1024,1024]{0,1:T(8,128)(2,1)} %copy.51) | copy-start | bytes 6291460
  639.1 16.8 %all-to-all-start.8 = ((bf16[64,2,1024]{2,1,0:T(2,128)(2,1)}), bf16[64,2,1024]{2,1,0:T(2,128)(2,1)S(1)}, u32[]{:S(2)}, u32[]{:S(2)}) async-start(bf16[64,2,1024]{2,1,0:T(2,128)(2,1)} %reshape.121), calls=%async_computation.8 | async-start | bytes 524288 | tf_op jit(solution)/shard_map/all_to_all | solution.py:39
  643.9 308.4 %all-reduce.5.cloned.1.call-start = ((), (), s32[]{:S(2)}) async-start(), calls=%async_computation.9 | async-start | bytes 16777216
  660.0 4.9 copy-start.6
  671.3 1.0 copy-start.7
  677.0 19.5 %all-to-all-start.5 = ((bf16[64,2,1024]{2,1,0:T(2,128)(2,1)}), bf16[64,2,1024]{2,1,0:T(2,128)(2,1)S(1)}, u32[]{:S(2)}, u32[]{:S(2)}) async-start(bf16[64,2,1024]{2,1,0:T(2,128)(2,1)} %reshape.115), calls=%async_computation.5 | async-start | bytes 524288 | tf_op jit(solution)/shard_map/all_to_all | solution.py:48
  697.9 257.1 %copy-start.1 = (bf16[512,1024]{1,0:T(8,128)(2,1)S(1)}, bf16[512,1024]{1,0:T(8,128)(2,1)}, u32[]{:S(2)}) copy-start(bf16[512,1024]{1,0:T(8,128)(2,1)} %param.13) | copy-start | bytes 3145732
Sparse Core Ops, SparseCore 0:
  671.4 280.8 all-reduce.4
where the time goes:
time: 971 us; the launch traced here: 962 us
  blocking collectives  383 us (39%)
  waiting for transfers between devices  283 us (29%)
  local copies, waits for them, and re-layouts  164 us (17%)
  starting transfers between devices  72.2 us (7%)
  matrix products  41.4 us (4%)
  between operations  14.7 us (2%)
    psum x3, blocking collectives, on_device(): total = lax.psum(jnp.sum(scaled, axis=(1, 2)), 'state')  383 us
    unnamed x2, waiting for transfers between devices  246 us
    unnamed x42, local copies, waits for them, and re-layouts  62.4 us
    all_to_all x3, starting transfers between devices, on_device(): lax.all_to_all(mixed, 'state', split_axis=2, concat_axis=1, tiled=True)  29 us
    all_to_all x3, starting transfers between devices, on_device(): lax.all_to_all(pulled, 'state', split_axis=1, concat_axis=2, tiled=True)  26.1 us
    all_to_all x6, local copies, waits for them, and re-layouts, on_device(): lax.all_to_all(pulled, 'state', split_axis=1, concat_axis=2, tiled=True)  24.6 us
    all_to_all x6, local copies, waits for them, and re-layouts, on_device(): lax.all_to_all(fresh, 'state', split_axis=1, concat_axis=2, tiled=True)  24.6 us
    all_to_all x6, local copies, waits for them, and re-layouts, on_device(): lax.all_to_all(mixed, 'state', split_axis=2, concat_axis=1, tiled=True)  24.1 us
  transfers between devices with their start and end apart: 10, of which 5 were waited for; matrix products, arithmetic and copies ran while one was open for 11% of the time, Pallas kernels for 0%

commit v1 on v0

--- a/solution.py
+++ b/solution.py
@@ -45,7 +45,10 @@
         )
         loglik = loglik + jnp.log(norm)
         fresh = (scaled / norm[:, None, None]).astype(jnp.bfloat16)
-        alpha = lax.all_to_all(fresh, "state", split_axis=1, concat_axis=2, tiled=True)
+        size = lax.axis_size("state")
+        parts = jnp.stack(jnp.split(fresh, size, axis=1), axis=0)
+        parts = lax.all_to_all(parts, "state", split_axis=0, concat_axis=0)
+        alpha = jnp.concatenate(parts, axis=2)
     factor = 1.0 / (seq_dev * lax.axis_size("dp") * STEPS)
     terms_rows = trans_rows.astype(f32) * sums_rows * factor
     terms_cols = trans_cols.astype(f32) * sums_cols * factor

time: 971 us -> 1090 us (1.12)
  local copies, waits for them, and re-layouts: 164 us -> 294 us
  waiting for transfers between devices: 283 us -> 265 us
    unnamed x42 -> x229, local copies, waits for them, and re-layouts: 62.4 us -> 188 us
    reshape x0 -> x6, local copies, waits for them, and re-layouts: none -> 24.6 us  [on_device(): alpha = jnp.concatenate(parts, axis=2)]
    all_to_all x6 -> x0, local copies, waits for them, and re-layouts: 24.6 us -> none  [on_device(): lax.all_to_all(fresh, 'state', split_axis=1, concat_axis=2, tiled=True)]
    another operation x0 -> x6, local copies, waits for them, and re-layouts: none -> 12.7 us  [on_device(): parts = jnp.stack(jnp.split(fresh, size, axis=1), axis=0)]
    unnamed x2, waiting for transfers between devices: 246 us -> 234 us
  transfers between devices with their start and end apart: 10 -> 10, of which waited for: 5 -> 4; matrix products, arithmetic and copies ran while one was open for 11% -> 19% of each run, Pallas kernels for 0% -> 0%
where the time goes in v1:
time: 1090 us; the launch traced here: 1080 us
  blocking collectives  384 us (35%)
  local copies, waits for them, and re-layouts  294 us (27%)
  waiting for transfers between devices  265 us (24%)
  starting transfers between devices  76.3 us (7%)
  matrix products  42 us (4%)
  between operations  15 us (1%)
    psum x3, blocking collectives, on_device(): total = lax.psum(jnp.sum(scaled, axis=(1, 2)), 'state')  384 us
    unnamed x2, waiting for transfers between devices  234 us
    unnamed x229, local copies, waits for them, and re-layouts  188 us
    all_to_all x3, starting transfers between devices, on_device(): lax.all_to_all(mixed, 'state', split_axis=2, concat_axis=1, tiled=True)  29 us
    all_to_all x3, starting transfers between devices, on_device(): lax.all_to_all(pulled, 'state', split_axis=1, concat_axis=2, tiled=True)  26.2 us
    all_to_all x6, local copies, waits for them, and re-layouts, on_device(): lax.all_to_all(pulled, 'state', split_axis=1, concat_axis=2, tiled=True)  24.6 us
    reshape x6, local copies, waits for them, and re-layouts, on_device(): alpha = jnp.concatenate(parts, axis=2)  24.6 us
    all_to_all x6, local copies, waits for them, and re-layouts, on_device(): lax.all_to_all(mixed, 'state', split_axis=2, concat_axis=1, tiled=True)  24.1 us
  transfers between devices with their start and end apart: 10, of which 4 were waited for; matrix products, arithmetic and copies ran while one was open for 19% of the time, Pallas kernels for 0%

profile of v1, /device:TPU:2, one launch (start us, length us, event | category | flops | bytes accessed | tf_op | source)
XLA Modules:
  0.0 1079.9 jit_solution(16945910652649583743)
XLA Ops:
  11.0 2.9 reshape.129
  14.0 12.1 %all-to-all-start = ((bf16[64,2,1024]{2,1,0:T(2,128)(2,1)}), bf16[64,2,1024]{2,1,0:T(2,128)(2,1)S(1)}, u32[]{:S(2)}, u32[]{:S(2)}) async-start(bf16[64,2,1024]{2,1,0:T(2,128)(2,1)} %reshape.129), calls=%async_computation | async-start | bytes 524288 | tf_op jit(solution)/shard_map/all_to_all | solution.py:29
  28.8 9.3 all-to-all-done
  42.2 4.8 all_to_all.90
  48.3 125.5 %psum.21 = f32[8]{0:T(128)S(1)} all-reduce(f32[8]{0:T(128)S(1)} %get-tuple-element.19), channel_id=1, replica_groups=mesh['dp'=4,'state'=64] {'state'}, use_global_device_ids=true, to_apply=%region_1.3 | all-reduce | flops 8 | bytes 64 | tf_op jit(solution)/shard_map/psum | solution.py:33
  218.4 3.2 copy.466
  221.5 2.9 reshape.131
  224.5 5.7 all-to-all-start.1
  233.4 8.6 all-to-all-done.1
  247.5 4.8 reshape.47
  255.3 4.4 reshape.133
  259.7 6.0 all-to-all-start.2
  270.3 3.9 copy.478
  279.3 4.4 reshape.141
  283.7 10.3 all-to-all-start.6
  296.5 4.3 copy.470
  300.7 4.7 all_to_all.95
  305.4 2.8 fusion.86
  308.3 129.0 %psum.22 = f32[8]{0:T(128)S(1)} all-reduce(f32[8]{0:T(128)S(1)} %get-tuple-element.21), channel_id=1, replica_groups=mesh['dp'=4,'state'=64] {'state'}, use_global_device_ids=true, to_apply=%region_3.5 | all-reduce | flops 8 | bytes 64 | tf_op jit(solution)/shard_map/psum | solution.py:33
  481.8 4.0 copy.471
  485.8 4.4 reshape.135
  490.2 4.9 all-to-all-start.3
  495.1 3.7 fusion.83
  501.3 4.3 copy.482
  505.6 5.3 all_to_all.105
  516.0 4.4 reshape.143
  520.3 10.9 %all-to-all-start.7 = ((bf16[64,2,1024]{2,1,0:T(2,128)(2,1)}), bf16[64,2,1024]{2,1,0:T(2,128)(2,1)S(1)}, u32[]{:S(2)}, u32[]{:S(2)}) async-start(bf16[64,2,1024]{2,1,0:T(2,128)(2,1)} %reshape.143), calls=%async_computation.7 | async-start | bytes 524288 | tf_op jit(solution)/shard_map/all_to_all | solution.py:39
  531.2 3.7 fusion.88
  537.3 4.3 copy.472
  541.6 4.7 reshape.49
  548.3 2.9 reshape.137
  551.3 10.9 %all-to-all-start.4 = ((bf16[64,2,1024]{2,1,0:T(2,128)(2,1)}), bf16[64,2,1024]{2,1,0:T(2,128)(2,1)}, u32[]{:S(2)}, u32[]{:S(2)}) async-start(bf16[64,2,1024]{2,1,0:T(2,128)(2,1)} %reshape.137), calls=%async_computation.4 | async-start | bytes 524288 | tf_op jit(solution)/shard_map/all_to_all | solution.py:29
  562.2 3.7 fusion.80
  570.0 4.7 all_to_all.109
  577.5 2.8 reshape.138
  583.0 4.8 all_to_all.100
  589.1 129.1 %psum.23 = f32[8]{0:T(128)S(1)} all-reduce(f32[8]{0:T(128)S(1)} %get-tuple-element.23), channel_id=1, replica_groups=mesh['dp'=4,'state'=64] {'state'}, use_global_device_ids=true, to_apply=%region_5.7 | all-reduce | flops 8 | bytes 64 | tf_op jit(solution)/shard_map/psum | solution.py:33
  722.1 2.9 reshape.145
  725.1 5.0 all-to-all-start.8
  763.1 6.5 fusion.4
  773.7 4.8 all_to_all.113
  778.6 6.4 fusion.2
  796.5 3.4 copy.476
  799.9 2.9 reshape.139
  802.9 10.6 all-to-all-start.5
  813.5 13.1 %all-to-all-done.5 = bf16[64,2,1024]{2,1,0:T(2,128)(2,1)S(1)} async-done(((bf16[64,2,1024]{2,1,0:T(2,128)(2,1)}), bf16[64,2,1024]{2,1,0:T(2,128)(2,1)S(1)}, u32[]{:S(2)}, u32[]{:S(2)}) %all-to-all-start.5) | async-done | bytes 262176 | tf_op jit(solution)/shard_map/all_to_all | solution.py:50
  830.7 5.4 reshape.51
  836.1 233.8 %all-reduce.5.cloned.1.call-done = (f32[1024,1024]{0,1:T(8,128)}, f32[1024,1024]{0,1:T(8,128)}) async-done(((f32[1024,1024]{0,1:T(8,128)}, f32[1024,1024]{0,1:T(8,128)}), (f32[1024,1024]{0,1:T(8,128)}, f32[1024,1024]{0,1:T(8,128)})) %all-reduce.5.cloned.1.call-update) | async-done | bytes 8388624
  (271 shorter events, 206.8 us)
Async XLA Ops:
  7.2 20.9 %copy-start = (bf16[512,1024]{1,0:T(8,128)(2,1)S(1)}, bf16[512,1024]{1,0:T(8,128)(2,1)}, u32[]{:S(2)}) copy-start(bf16[512,1024]{1,0:T(8,128)(2,1)} %param.13) | copy-start | bytes 3145732
  9.4 16.7 %copy-start.8 = (s32[8,3]{0,1:T(4,128)S(1)}, s32[8,3]{0,1:T(4,128)}, u32[]{:S(2)}) copy-start(s32[8,3]{0,1:T(4,128)} %param.10) | copy-start | bytes 292
  14.0 24.1 %all-to-all-start = ((bf16[64,2,1024]{2,1,0:T(2,128)(2,1)}), bf16[64,2,1024]{2,1,0:T(2,128)(2,1)S(1)}, u32[]{:S(2)}, u32[]{:S(2)}) async-start(bf16[64,2,1024]{2,1,0:T(2,128)(2,1)} %reshape.129), calls=%async_computation | async-start | bytes 524288 | tf_op jit(solution)/shard_map/all_to_all | solution.py:29
  42.2 4.9 copy-start.3
  224.5 17.5 %all-to-all-start.1 = ((bf16[64,2,1024]{2,1,0:T(2,128)(2,1)}), bf16[64,2,1024]{2,1,0:T(2,128)(2,1)}, u32[]{:S(2)}, u32[]{:S(2)}) async-start(bf16[64,2,1024]{2,1,0:T(2,128)(2,1)} %reshape.131), calls=%async_computation.1 | async-start | bytes 524288 | tf_op jit(solution)/shard_map/all_to_all | solution.py:50
  247.5 4.9 copy-start.2
  259.7 24.0 %all-to-all-start.2 = ((bf16[64,2,1024]{2,1,0:T(2,128)(2,1)}), bf16[64,2,1024]{2,1,0:T(2,128)(2,1)S(1)}, u32[]{:S(2)}, u32[]{:S(2)}) async-start(bf16[64,2,1024]{2,1,0:T(2,128)(2,1)} %reshape.133), calls=%async_computation.2 | async-start | bytes 524288 | tf_op jit(solution)/shard_map/all_to_all | solution.py:29
  283.7 206.5 %all-to-all-start.6 = ((bf16[64,2,1024]{2,1,0:T(2,128)(2,1)}), bf16[64,2,1024]{2,1,0:T(2,128)(2,1)S(1)}, u32[]{:S(2)}, u32[]{:S(2)}) async-start(bf16[64,2,1024]{2,1,0:T(2,128)(2,1)} %reshape.141), calls=%async_computation.6 | async-start | bytes 524288 | tf_op jit(solution)/shard_map/all_to_all | solution.py:39
  490.2 30.1 %all-to-all-start.3 = ((bf16[64,2,1024]{2,1,0:T(2,128)(2,1)}), bf16[64,2,1024]{2,1,0:T(2,128)(2,1)S(1)}, u32[]{:S(2)}, u32[]{:S(2)}) async-start(bf16[64,2,1024]{2,1,0:T(2,128)(2,1)} %reshape.135), calls=%async_computation.3 | async-start | bytes 524288 | tf_op jit(solution)/shard_map/all_to_all | solution.py:50
  513.5 17.8 %copy-start.7 = (bf16[8,16,1024]{2,1,0:T(8,128)(2,1)S(1)}, bf16[8,16,1024]{2,1,0:T(8,128)(2,1)}, u32[]{:S(2)}) copy-start(bf16[8,16,1024]{2,1,0:T(8,128)(2,1)} %param.9) | copy-start | bytes 786436
  520.3 31.0 %all-to-all-start.7 = ((bf16[64,2,1024]{2,1,0:T(2,128)(2,1)}), bf16[64,2,1024]{2,1,0:T(2,128)(2,1)S(1)}, u32[]{:S(2)}, u32[]{:S(2)}) async-start(bf16[64,2,1024]{2,1,0:T(2,128)(2,1)} %reshape.143), calls=%async_computation.7 | async-start | bytes 524288 | tf_op jit(solution)/shard_map/all_to_all | solution.py:39
  551.3 26.2 %all-to-all-start.4 = ((bf16[64,2,1024]{2,1,0:T(2,128)(2,1)}), bf16[64,2,1024]{2,1,0:T(2,128)(2,1)}, u32[]{:S(2)}, u32[]{:S(2)}) async-start(bf16[64,2,1024]{2,1,0:T(2,128)(2,1)} %reshape.137), calls=%async_computation.4 | async-start | bytes 524288 | tf_op jit(solution)/shard_map/all_to_all | solution.py:29
  583.0 4.9 copy-start.4
  725.1 38.0 %copy-start.5 = (bf16[1024,1024]{0,1:T(8,128)(2,1)S(1)}, bf16[1024,1024]{0,1:T(8,128)(2,1)}, u32[]{:S(2)}) copy-start(bf16[1024,1024]{0,1:T(8,128)(2,1)} %copy.478) | copy-start | bytes 6291460
  725.1 44.5 %all-to-all-start.8 = ((bf16[64,2,1024]{2,1,0:T(2,128)(2,1)}), bf16[64,2,1024]{2,1,0:T(2,128)(2,1)S(1)}, u32[]{:S(2)}, u32[]{:S(2)}) async-start(bf16[64,2,1024]{2,1,0:T(2,128)(2,1)} %reshape.145), calls=%async_computation.8 | async-start | bytes 524288 | tf_op jit(solution)/shard_map/all_to_all | solution.py:39
  730.0 339.9 %all-reduce.5.cloned.1.call-start = ((), (), s32[]{:S(2)}) async-start(), calls=%async_computation.9 | async-start | bytes 16777216
  773.7 4.9 copy-start.6
  802.9 23.7 %all-to-all-start.5 = ((bf16[64,2,1024]{2,1,0:T(2,128)(2,1)}), bf16[64,2,1024]{2,1,0:T(2,128)(2,1)S(1)}, u32[]{:S(2)}, u32[]{:S(2)}) async-start(bf16[64,2,1024]{2,1,0:T(2,128)(2,1)} %reshape.139), calls=%async_computation.5 | async-start | bytes 524288 | tf_op jit(solution)/shard_map/all_to_all | solution.py:50
  828.0 244.6 %copy-start.1 = (bf16[512,1024]{1,0:T(8,128)(2,1)S(1)}, bf16[512,1024]{1,0:T(8,128)(2,1)}, u32[]{:S(2)}) copy-start(bf16[512,1024]{1,0:T(8,128)(2,1)} %param.13) | copy-start | bytes 3145732
Sparse Core Ops, SparseCore 0:
  785.2 284.7 all-reduce.4
